TPU v7x, 768 devices: a whole 4x8x12 slice. The times are simulated.
768 devices in a mesh: fsdp: 96 (over y_hi, z, core), col: 8 (over y_lo, x).
Axes of the slice: x: 4, y: 8 (y_hi: 4, y_lo: 2; y = y_hi * 2 + y_lo), z: 12, core: 2. Of those that a mesh axis runs over, the one named last changes fastest.
Arguments:
- grad: bfloat16 [7680, 18432], P('fsdp', 'col'), may hold values from -20 to 20
- basis: bfloat16 [7680, 512], P('fsdp', 'col'), may hold values from -0.25 to 0.25
- exp_avg: float32 [8, 2304, 512], P('col', 'fsdp'), may hold values from -6 to 6
- exp_avg_sq: float32 [8, 2304, 512], P('col', 'fsdp'), may hold values from 0.05 to 5
- step: int32 [1], replicated, may hold values from 1 to 8
Outputs:
- update: bfloat16 [7680, 18432], P('fsdp', 'col')
- new_avg: float32 [8, 2304, 512], P('col', 'fsdp')
- new_sq: float32 [8, 2304, 512], P('col', 'fsdp')
All inputs are finite; a program needn't handle non-finite values.
Results may differ from a plain program's by a relative error of at most 0.0049.
Values may be sent and summed in bfloat16 or wider, within the bound.
No kernel may reach another device: no remote copies, remote signals or barrier semaphores. Data moves between devices by JAX's collectives and lax.ppermute only.
A program may use at most 32 MiB of HBM per device.

v0:
```python
import jax
import jax.numpy as jnp
from jax import lax
from jax.sharding import PartitionSpec as P

beta_one = 0.9
beta_two = 0.999
adam_eps = 1e-08


def adam_moments(low, exp_avg, exp_avg_sq, step):
    new_avg = beta_one * exp_avg + (1.0 - beta_one) * low
    new_sq = beta_two * exp_avg_sq + (1.0 - beta_two) * low * low
    count = step[0].astype(jnp.float32)
    first_fix = 1.0 - jnp.power(jnp.float32(beta_one), count)
    second_fix = 1.0 - jnp.power(jnp.float32(beta_two), count)
    normalized = (new_avg / first_fix / (jnp.sqrt(new_sq / second_fix) + adam_eps)).astype(
        jnp.bfloat16
    )
    return (new_avg, new_sq, normalized)


def local(grad, basis, exp_avg, exp_avg_sq, step):
    col_rows = exp_avg.shape[1]
    rank = exp_avg.shape[2]
    full_basis = lax.all_gather(basis, "col", axis=1, tiled=True)
    low = lax.psum_scatter(
        lax.dot_general(
            grad, full_basis, (((0,), (0,)), ((), ())), preferred_element_type=jnp.float32
        ),
        "fsdp",
        scatter_dimension=0,
        tiled=True,
    )
    new_avg, new_sq, normalized = adam_moments(
        low.reshape(exp_avg.shape), exp_avg, exp_avg_sq, step
    )
    update = lax.dot_general(
        full_basis,
        lax.all_gather(normalized.reshape(col_rows, rank), "fsdp", axis=0, tiled=True),
        (((1,), (1,)), ((), ())),
        preferred_element_type=jnp.float32,
    )
    return (update.astype(jnp.bfloat16), new_avg, new_sq)


def solution(mesh):
    return jax.shard_map(
        local,
        mesh=mesh,
        in_specs=(
            P("fsdp", "col"),
            P("fsdp", "col"),
            P("col", "fsdp", None),
            P("col", "fsdp", None),
            P(),
        ),
        out_specs=(P("fsdp", "col"), P("col", "fsdp", None), P("col", "fsdp", None)),
        check_vma=False,
    )
```

profile of v0, /device:TPU:1, one launch (start us, length us, event | category | flops | bytes accessed | tf_op | source)
XLA Modules:
  0.0 393.6 jit_solution(2822810730638512891)
XLA Ops:
  7.2 0.0 copy-start
  7.2 0.0 reduce-scatter.2.cloned.1.call-start
  7.2 23.4 %all_gather.6 = bf16[80,512]{0,1:T(8,128)(2,1)S(1)} all-gather(bf16[80,64]{0,1:T(8,128)(2,1)} %param.6), channel_id=1, replica_groups=mesh['fsdp'=96,'col'=8] {'col'}, dimensions={1}, use_global_device_ids=true | all-gather | bytes 92160 | tf_op jit(solution)/shard_map/all_gather | solution.py:26
  30.7 0.0 copy-done
  30.7 2.9 fusion.5
  33.6 0.0 copy-start.1
  33.6 0.0 copy-start.2
  33.6 0.0 reduce-scatter.2.cloned.1.call-update
  33.6 0.0 all-gather.3.cloned.1.call-start
  34.4 222.8 %reduce-scatter.2.cloned.1.call-done = f32[24,512]{1,0:T(8,128)} async-done(((f32[2304,512]{1,0:T(8,128)}), f32[24,512]{1,0:T(8,128)}) %reduce-scatter.2.cloned.1.call-update) | async-done | bytes 49168 | tf_op jit(solution)/shard_map/reduce_scatter | solution.py:27
  257.2 0.0 copy-done.1
  257.2 0.0 copy-done.2
  257.2 1.5 divide_convert_fusion
  258.6 0.0 all-gather.3.cloned.1.call-update
  258.7 124.8 %all-gather.3.cloned.1.call-done = bf16[1,2304,512]{2,1,0:T(8,128)(2,1)} async-done(((bf16[1,24,512]{2,1,0:T(8,128)(2,1)}), bf16[1,2304,512]{2,1,0:T(8,128)(2,1)}) %all-gather.3.cloned.1.call-update) | async-done | bytes 2359312 | tf_op jit(solution)/shard_map/all_gather | solution.py:40
  383.5 3.3 fusion
Async XLA Ops:
  7.2 23.5 %copy-start = (bf16[80,2304]{1,0:T(8,128)(2,1)S(1)}, bf16[80,2304]{1,0:T(8,128)(2,1)}, u32[]{:S(2)}) copy-start(bf16[80,2304]{1,0:T(8,128)(2,1)} %param.5) | copy-start | bytes 1105924
  7.2 250.0 %reduce-scatter.2.cloned.1.call-start = ((), (), s32[]{:S(2)}) async-start(), calls=%async_computation.1 | async-start | bytes 4767744 | tf_op jit(solution)/shard_map/reduce_scatter | solution.py:27
  33.6 223.6 %copy-start.1 = (f32[1,24,512]{2,1,0:T(8,128)S(1)}, f32[1,24,512]{2,1,0:T(8,128)}, u32[]{:S(2)}) copy-start(f32[1,24,512]{2,1,0:T(8,128)} %param.8) | copy-start | bytes 147460
  33.6 223.6 %copy-start.2 = (f32[1,24,512]{2,1,0:T(8,128)S(1)}, f32[1,24,512]{2,1,0:T(8,128)}, u32[]{:S(2)}) copy-start(f32[1,24,512]{2,1,0:T(8,128)} %param.7) | copy-start | bytes 147460
  33.6 349.8 %all-gather.3.cloned.1.call-start = ((), (), s32[]{:S(2)}) async-start(), calls=%async_computation.2 | async-start | bytes 2383872 | tf_op jit(solution)/shard_map/all_gather | solution.py:40
Sparse Core Ops, SparseCore 0:
  33.8 223.3 reduce-scatter.1
  261.4 122.0 all-gather.2
where the time goes:
time: 394 us
  waiting for transfers between devices  348 us (88%)
  blocking collectives  23.4 us (6%)
  between operations  14.8 us (4%)
  matrix products  6.2 us (2%)
    reduce_scatter x1, waiting for transfers between devices, local(): lax.psum_scatter(lax.dot_general(grad, full_basis, (((0,), (0,)), ((), ()...  223 us
    all_gather x1, waiting for transfers between devices, local(): lax.all_gather(normalized.reshape(col_rows, rank), 'fsdp', axis=0, tiled=...  125 us
    all_gather x1, blocking collectives, local(): full_basis = lax.all_gather(basis, 'col', axis=1, tiled=True)  23.4 us
  transfers between devices with their start and end apart: 2, of which 2 were waited for; matrix products, arithmetic and copies ran while one was open for 0% of the time, Pallas kernels for 0%

commit v1 on v0

v1 whole, which is shorter than its diff:
```python
import jax
import jax.numpy as jnp
from jax import lax
from jax.sharding import PartitionSpec as P

beta_one = 0.9
beta_two = 0.999
adam_eps = 1e-08

FSDP = ("yh", "zh", "zl", "c")
COL = ("yl", "x")
INNER = ("yh", "zh")
OUTER = ("zl", "c")


def exchange(x, axes):
    return lax.all_to_all(x, axes, split_axis=0, concat_axis=0, tiled=True)


def to_all(x, count):
    return jnp.broadcast_to(x[None], (count,) + x.shape)


def adam_moments(low, exp_avg, exp_avg_sq, step):
    new_avg = beta_one * exp_avg + (1.0 - beta_one) * low
    new_sq = beta_two * exp_avg_sq + (1.0 - beta_two) * low * low
    count = step[0].astype(jnp.float32)
    first_fix = 1.0 - jnp.power(jnp.float32(beta_one), count)
    second_fix = 1.0 - jnp.power(jnp.float32(beta_two), count)
    normalized = (new_avg / first_fix / (jnp.sqrt(new_sq / second_fix) + adam_eps)).astype(
        jnp.bfloat16
    )
    return (new_avg, new_sq, normalized)


def local(grad, basis, exp_avg, exp_avg_sq, step):
    rows, cols = grad.shape
    part = basis.shape[1]
    own = exp_avg.shape[1]
    rank = exp_avg.shape[2]
    n_col = rank // part
    n_outer = 8
    n_inner = cols // own // n_outer
    wide = cols // n_inner
    tall = rows * n_inner
    half = tall // 2
    blocks = grad.reshape(rows, n_inner, wide).transpose(1, 0, 2)
    got = exchange(jnp.concatenate([blocks, to_all(basis, n_inner)], axis=2), INNER)
    got = got.reshape(tall, wide + part)
    piece = got[:, wide:]
    folded = jnp.concatenate([piece[:half], piece[half:]], axis=1)
    folded = exchange(to_all(folded, n_col), COL)
    full = jnp.concatenate(
        [
            folded[:, :, :part].transpose(1, 0, 2).reshape(half, rank),
            folded[:, :, part:].transpose(1, 0, 2).reshape(half, rank),
        ],
        axis=0,
    )
    partial = lax.dot_general(
        got[:, :wide], full, (((0,), (0,)), ((), ())), preferred_element_type=jnp.float32
    )
    sums = exchange(partial.astype(jnp.bfloat16).reshape(n_outer, own, rank), OUTER)
    low = jnp.sum(sums.astype(jnp.float32), axis=0)
    new_avg, new_sq, normalized = adam_moments(
        low.reshape(exp_avg.shape), exp_avg, exp_avg_sq, step
    )
    normalized = exchange(to_all(normalized[0], n_outer), OUTER).reshape(wide, rank)
    update = lax.dot_general(
        full, normalized, (((1,), (1,)), ((), ())), preferred_element_type=jnp.float32
    ).astype(jnp.bfloat16)
    update = update.reshape(n_inner, rows, wide)
    even = jnp.concatenate(
        [
            update[:, :, :128],
            jnp.concatenate([update[:, : rows // 2, 128:], update[:, rows // 2 :, 128:]], axis=2),
        ],
        axis=1,
    )
    even = exchange(even, INNER)
    tail = even[:, rows:]
    update = jnp.concatenate(
        [
            even[:, :rows],
            jnp.concatenate([tail[:, :, :64], tail[:, :, 64:]], axis=1),
        ],
        axis=2,
    )
    update = update.transpose(1, 0, 2).reshape(rows, cols)
    return (update, new_avg, new_sq)


def solution(mesh):
    split = jax.sharding.Mesh(mesh.devices.reshape(4, 3, 4, 2, 2, 4), FSDP + COL)
    return jax.shard_map(
        local,
        mesh=split,
        in_specs=(
            P(FSDP, COL),
            P(FSDP, COL),
            P(COL, FSDP, None),
            P(COL, FSDP, None),
            P(),
        ),
        out_specs=(P(FSDP, COL), P(COL, FSDP, None), P(COL, FSDP, None)),
        check_vma=False,
    )
```

time: 394 us -> 123 us (0.31)
  waiting for transfers between devices: 348 us -> 5.73 us
  blocking collectives: 23.4 us -> 88.9 us
  starting transfers between devices: 0.08 us -> 18 us
  between operations: 14.8 us -> 1.54 us
  local copies, waits for them, and re-layouts: 0.02 us -> 5.07 us
  matrix products: 6.2 us -> 1.83 us
    reduce_scatter x1 -> x0, waiting for transfers between devices: 223 us -> none  [local(): lax.psum_scatter(lax.dot_general(grad, full_basis, (((0,), (0,)), ((), ()...]
    all_gather x1 -> x0, waiting for transfers between devices: 125 us -> none  [local(): lax.all_gather(normalized.reshape(col_rows, rank), 'fsdp', axis=0, tiled=...]
    all_to_all x0 -> x4, blocking collectives: none -> 88.9 us  [exchange(): return lax.all_to_all(x, axes, split_axis=0, concat_axis=0, tiled=True)]
    all_gather x1 -> x0, blocking collectives: 23.4 us -> none  [local(): full_basis = lax.all_gather(basis, 'col', axis=1, tiled=True)]
    all_to_all x0 -> x1, starting transfers between devices: none -> 18 us  [exchange(): return lax.all_to_all(x, axes, split_axis=0, concat_axis=0, tiled=True)]
    all_to_all x0 -> x1, waiting for transfers between devices: none -> 5.73 us  [exchange(): return lax.all_to_all(x, axes, split_axis=0, concat_axis=0, tiled=True)]
    dot_general x2, matrix products: 6.2 us -> 1.83 us  [the longest x1 1.38 us: local(): lax.dot_general(got[:, :wide], full, (((0,), (0,)), ((), ())), preferred_...]
  transfers between devices with their start and end apart: 2 -> 1, of which waited for: 2 -> 1; matrix products, arithmetic and copies ran while one was open for 0% -> 0% of each run, Pallas kernels for 0% -> 0%
where the time goes in v1:
time: 123 us; the launch traced here: 122 us
  blocking collectives  88.9 us (72%)
  starting transfers between devices  18 us (15%)
  waiting for transfers between devices  5.73 us (5%)
  local copies, waits for them, and re-layouts  5.07 us (4%)
  matrix products  1.83 us (1%)
  between operations  1.54 us (1%)
  other arithmetic  1.25 us (1%)
    all_to_all x4, blocking collectives, exchange(): return lax.all_to_all(x, axes, split_axis=0, concat_axis=0, tiled=True)  88.9 us
    all_to_all x1, starting transfers between devices, exchange(): return lax.all_to_all(x, axes, split_axis=0, concat_axis=0, tiled=True)  18 us
    all_to_all x1, waiting for transfers between devices, exchange(): return lax.all_to_all(x, axes, split_axis=0, concat_axis=0, tiled=True)  5.73 us
  transfers between devices with their start and end apart: 1, of which 1 were waited for; matrix products, arithmetic and copies ran while one was open for 0% of the time, Pallas kernels for 0%

profile of v1, /device:TPU:1, one launch (start us, length us, event | category | flops | bytes accessed | tf_op | source)
XLA Modules:
  0.0 122.3 jit_solution(9890149314889911125)
XLA Ops:
  0.6 0.0 copy-start.2
  0.6 1.6 %reshape.62 = bf16[80,12,192]{2,1,0:T(8,128)(2,1)S(1)} reshape(bf16[80,2304]{1,0:T(8,128)(2,1)} %param.5) | data formatting | bytes 737280 | tf_op jit(solution)/shard_map/reshape | solution.py:47
  2.3 0.0 copy-done.2
  2.3 0.1 copy.15
  2.4 0.1 broadcast_in_dim.8
  2.4 0.2 pad_maximum_fusion.3
  2.7 0.1 copy.16
  2.8 39.2 %all_to_all.25 = bf16[12,80,256]{2,1,0:T(8,128)(2,1)S(1)} all-to-all(bf16[12,80,256]{2,1,0:T(8,128)(2,1)S(1)} %copy.16), channel_id=1, replica_groups=mesh['yh'=4,'zh'=3,'zl'=4,'c'=2,'yl'=2,'x'=4] {'yh','zh'}, dimensions={0} | all-to-all | bytes 983040 | tf_op jit(solution)/shard_map/all_to_all | solution.py:17
  42.0 0.1 fusion.9
  42.1 0.1 pad_maximum_fusion.4
  42.2 0.1 broadcast_in_dim.9
  42.4 14.4 %all_to_all.26 = bf16[8,480,128]{2,1,0:T(8,128)(2,1)S(1)} all-to-all(bf16[8,480,128]{2,1,0:T(8,128)(2,1)S(1)} %broadcast_in_dim.9), channel_id=1, replica_groups=mesh['yh'=4,'zh'=3,'zl'=4,'c'=2,'yl'=2,'x'=4] {'yl','x'}, dimensions={0} | all-to-all | bytes 1966080 | tf_op jit(solution)/shard_map/all_to_all | solution.py:17
  56.7 0.4 slice_bitcast_fusion.1
  57.1 0.3 copy.17
  57.4 0.3 copy.18
  57.8 0.0 copy-start
  57.8 0.0 copy-start.1
  57.8 1.4 %convolution_convert_fusion.1 = bf16[192,512]{1,0:T(8,128)(2,1)} fusion(bf16[480,512]{0,1:T(8,128)(2,1)S(1)} %bitcast.32, bf16[480,512]{0,1:T(8,128)(2,1)S(1)} %bitcast.30, bf16[960,256]{1,0:T(8,128)(2,1)S(1)} %bitcast.29), kind=kOutput, calls=%fused_computation.1 | convolution fusion | flops 190808064 | bytes 1671168 | tf_op jit(solution)/shard_map/dot_general | solution.py:60
  59.2 18.0 %all-to-all-start.2 = ((bf16[8,24,512]{2,1,0:T(8,128)(2,1)}), bf16[8,24,512]{2,1,0:T(8,128)(2,1)S(1)}, u32[]{:S(2)}, u32[]{:S(2)}) async-start(bf16[8,24,512]{2,1,0:T(8,128)(2,1)} %bitcast.6), calls=%async_computation.2 | async-start | bytes 393216 | tf_op jit(solution)/shard_map/all_to_all | solution.py:17
  77.9 5.7 %all-to-all-done.2 = bf16[8,24,512]{2,1,0:T(8,128)(2,1)S(1)} async-done(((bf16[8,24,512]{2,1,0:T(8,128)(2,1)}), bf16[8,24,512]{2,1,0:T(8,128)(2,1)S(1)}, u32[]{:S(2)}, u32[]{:S(2)}) %all-to-all-start.2) | async-done | bytes 196640 | tf_op jit(solution)/shard_map/all_to_all | solution.py:17
  83.7 0.0 copy-done
  83.7 0.0 copy-done.1
  83.7 0.7 fusion.3
  84.4 10.7 %all_to_all.27 = bf16[8,24,512]{2,1,0:T(8,128)(2,1)S(1)} all-to-all(bf16[8,24,512]{2,1,0:T(8,128)(2,1)S(1)} %broadcast_in_dim.22), channel_id=1, replica_groups=mesh['yh'=4,'zh'=3,'zl'=4,'c'=2,'yl'=2,'x'=4] {'zl','c'}, dimensions={0} | all-to-all | bytes 393216 | tf_op jit(solution)/shard_map/all_to_all | solution.py:17
  95.1 0.4 convolution_convert_fusion
  95.6 0.2 copy.19
  95.9 0.1 maximum_maximum_fusion
  96.0 24.6 %all_to_all.28 = bf16[12,120,128]{2,1,0:T(8,128)(2,1)S(1)} all-to-all(bf16[12,120,128]{2,1,0:T(8,128)(2,1)S(1)} %maximum_maximum_fusion), channel_id=1, replica_groups=mesh['yh'=4,'zh'=3,'zl'=4,'c'=2,'yl'=2,'x'=4] {'yh','zh'}, dimensions={0} | all-to-all | bytes 737280 | tf_op jit(solution)/shard_map/all_to_all | solution.py:17
  120.6 0.1 fusion.10
  120.8 0.1 maximum_bitcast_fusion
  120.9 0.2 copy.20
  121.0 1.3 %reshape.69 = bf16[80,2304]{1,0:T(8,128)(2,1)} reshape(bf16[80,12,192]{2,1,0:T(8,128)(2,1)S(1)} %copy.20) | data formatting | bytes 737280 | tf_op jit(solution)/shard_map/reshape | solution.py:89
  (5 shorter events, 0.1 us)
Async XLA Ops:
  0.6 1.6 %copy-start.2 = (bf16[80,64]{0,1:T(8,128)(2,1)S(1)}, bf16[80,64]{0,1:T(8,128)(2,1)}, u32[]{:S(2)}) copy-start(bf16[80,64]{0,1:T(8,128)(2,1)} %param.6) | copy-start | bytes 30724
  57.8 25.9 %copy-start = (f32[1,24,512]{2,1,0:T(8,128)S(1)}, f32[1,24,512]{2,1,0:T(8,128)}, u32[]{:S(2)}) copy-start(f32[1,24,512]{2,1,0:T(8,128)} %param.8) | copy-start | bytes 147460
  57.8 25.9 %copy-start.1 = (f32[1,24,512]{2,1,0:T(8,128)S(1)}, f32[1,24,512]{2,1,0:T(8,128)}, u32[]{:S(2)}) copy-start(f32[1,24,512]{2,1,0:T(8,128)} %param.7) | copy-start | bytes 147460
  59.2 24.5 %all-to-all-start.2 = ((bf16[8,24,512]{2,1,0:T(8,128)(2,1)}), bf16[8,24,512]{2,1,0:T(8,128)(2,1)S(1)}, u32[]{:S(2)}, u32[]{:S(2)}) async-start(bf16[8,24,512]{2,1,0:T(8,128)(2,1)} %bitcast.6), calls=%async_computation.2 | async-start | bytes 393216 | tf_op jit(solution)/shard_map/all_to_all | solution.py:17

commit v2 on v1

v2 whole, which is shorter than its diff:
```python
import jax
import jax.numpy as jnp
from jax import lax
from jax.sharding import PartitionSpec as P

beta_one = 0.9
beta_two = 0.999
adam_eps = 1e-08

FSDP = ("y", "z", "core")
COL = ("y_lo", "x")
INNER = ("y", "core")
OUTER = ("z",)
N_Y, N_Z, N_CORE = 4, 12, 2
N_INNER = N_Y * N_CORE
N_OUTER = N_Z
N_COL = 8
LANES = 128


def exchange(x, axes):
    return lax.all_to_all(x, axes, split_axis=0, concat_axis=0, tiled=True)


def to_all(x, count):
    return jnp.broadcast_to(x[None], (count,) + x.shape)


def local(grad, basis, exp_avg, exp_avg_sq, step):
    rows, cols = grad.shape
    part = basis.shape[1]
    own, rank = exp_avg.shape[1:]
    wide = cols // N_INNER
    tall = rows * N_INNER
    half = tall // 2
    count = step[0].astype(jnp.float32)
    first_fix = 1.0 - jnp.power(jnp.float32(beta_one), count)
    second_fix = 1.0 - jnp.power(jnp.float32(beta_two), count)
    grad, basis, first_fix, second_fix = lax.optimization_barrier(
        (grad, basis, first_fix, second_fix)
    )

    blocks = grad.reshape(rows, N_Y, N_Z, N_CORE, own).transpose(1, 3, 0, 2, 4)
    blocks = blocks.reshape(N_INNER, rows, wide)
    got = exchange(jnp.concatenate([blocks, to_all(basis, N_INNER)], axis=2), INNER)
    got = got.reshape(tall, wide + part)

    piece = got[:, wide:]
    folded = jnp.concatenate([piece[:half], piece[half:]], axis=1)
    folded = exchange(to_all(folded, N_COL), COL)
    full = jnp.concatenate(
        [
            folded[:, :, :part].transpose(1, 0, 2).reshape(half, rank),
            folded[:, :, part:].transpose(1, 0, 2).reshape(half, rank),
        ],
        axis=0,
    )

    partial = lax.dot_general(
        got[:, :wide], full, (((0,), (0,)), ((), ())), preferred_element_type=jnp.float32
    )
    sums = exchange(partial.astype(jnp.bfloat16).reshape(N_OUTER, own, rank), OUTER)
    low = jnp.sum(sums.astype(jnp.float32), axis=0).reshape(exp_avg.shape)
    new_avg = beta_one * exp_avg + (1.0 - beta_one) * low
    new_sq = beta_two * exp_avg_sq + (1.0 - beta_two) * low * low
    normalized = (new_avg / first_fix / (jnp.sqrt(new_sq / second_fix) + adam_eps)).astype(
        jnp.bfloat16
    )

    normalized = exchange(to_all(normalized[0], N_OUTER), OUTER).reshape(wide, rank)
    update = lax.dot_general(
        full, normalized, (((1,), (1,)), ((), ())), preferred_element_type=jnp.float32
    ).astype(jnp.bfloat16)
    update = update.reshape(N_INNER, rows, wide)
    narrow = wide - 2 * LANES
    folds = LANES // narrow
    deep = -(-rows // (8 * folds)) * 8
    tail = jnp.pad(update[:, :, 2 * LANES :], ((0, 0), (0, folds * deep - rows), (0, 0)))
    tail = [tail[:, deep * k : deep * (k + 1)] for k in range(folds)]
    packed = jnp.concatenate(
        [update[:, :, :LANES], update[:, :, LANES : 2 * LANES], jnp.concatenate(tail, axis=2)],
        axis=1,
    )
    packed = exchange(packed, INNER)
    tail = packed[:, 2 * rows :]
    tail = [tail[:, :, narrow * k : narrow * (k + 1)] for k in range(folds)]
    tail = jnp.concatenate(tail, axis=1)[:, :rows]
    update = jnp.concatenate([packed[:, :rows], packed[:, rows : 2 * rows], tail], axis=2)
    update = update.reshape(N_Y, N_CORE, rows, N_Z, own).transpose(2, 0, 3, 1, 4)
    return (update.reshape(rows, cols), new_avg, new_sq)


def solution(mesh):
    split = jax.sharding.Mesh(mesh.devices.reshape(N_Y, N_Z, N_CORE, 2, 4), FSDP + COL)
    return jax.shard_map(
        local,
        mesh=split,
        in_specs=(
            P(FSDP, COL),
            P(FSDP, COL),
            P(COL, FSDP, None),
            P(COL, FSDP, None),
            P(),
        ),
        out_specs=(P(FSDP, COL), P(COL, FSDP, None), P(COL, FSDP, None)),
        check_vma=False,
    )
```

time: 123 us -> 114 us (0.927)
  starting transfers between devices: 18 us -> 0 us
  blocking collectives: 88.9 us -> 105 us
  waiting for transfers between devices: 5.73 us -> 0 us
    all_to_all x1 -> x0, starting transfers between devices: 18 us -> none  [exchange(): return lax.all_to_all(x, axes, split_axis=0, concat_axis=0, tiled=True)]
    all_to_all x4 -> x5, blocking collectives: 88.9 us -> 105 us  [exchange(): return lax.all_to_all(x, axes, split_axis=0, concat_axis=0, tiled=True)]
    all_to_all x1 -> x0, waiting for transfers between devices: 5.73 us -> none  [exchange(): return lax.all_to_all(x, axes, split_axis=0, concat_axis=0, tiled=True)]
    reshape x2 -> x0, local copies, waits for them, and re-layouts: 2.88 us -> none  [the longest x1 1.61 us: local(): blocks = grad.reshape(rows, n_inner, wide).transpose(1, 0, 2)]
    unnamed x7, local copies, waits for them, and re-layouts: 0.11 us -> 1.64 us
    optimization_barrier x0 -> x1, local copies, waits for them, and re-layouts: none -> 1.31 us  [local(): lax.optimization_barrier((grad, basis, first_fix, second_fix))]
  transfers between devices with their start and end apart: 1 -> 0, of which waited for: 1 -> 0; matrix products, arithmetic and copies ran while one was open for 0% -> 0% of each run, Pallas kernels for 0% -> 0%
where the time goes in v2:
time: 114 us
  blocking collectives  105 us (92%)
  local copies, waits for them, and re-layouts  5.32 us (5%)
  between operations  1.55 us (1%)
    all_to_all x5, blocking collectives, exchange(): return lax.all_to_all(x, axes, split_axis=0, concat_axis=0, tiled=True)  105 us

profile of v2, /device:TPU:1, one launch (start us, length us, event | category | flops | bytes accessed | tf_op | source)
XLA Modules:
  0.0 114.0 jit_solution(17422211077276913150)
XLA Ops:
  1.4 1.3 %copy.37 = bf16[80,2304]{0,1:T(8,128)(2,1)S(1)} copy(bf16[80,2304]{1,0:T(8,128)(2,1)} %param.5) | data formatting | bytes 737280 | tf_op jit(solution)/shard_map/optimization_barrier | solution.py:39
  2.7 0.0 copy-start.2
  2.7 0.1 copy.38
  2.8 0.6 copy-done.2
  3.4 0.1 pad_maximum_fusion
  3.6 0.3 copy.39
  3.9 26.9 %all_to_all.25 = bf16[8,80,352]{2,1,0:T(8,128)(2,1)S(1)} all-to-all(bf16[8,80,352]{2,1,0:T(8,128)(2,1)S(1)} %copy.39), channel_id=1, replica_groups=mesh['y'=4,'z'=12,'core'=2,'y_lo'=2,'x'=4] {'y','core'}, dimensions={0} | all-to-all | bytes 901120 | tf_op jit(solution)/shard_map/all_to_all | solution.py:22
  30.8 0.1 fusion.11
  30.9 0.1 pad_maximum_fusion.7
  31.0 0.1 broadcast_in_dim.9
  31.1 12.4 %all_to_all.26 = bf16[8,320,128]{2,1,0:T(8,128)(2,1)S(1)} all-to-all(bf16[8,320,128]{2,1,0:T(8,128)(2,1)S(1)} %broadcast_in_dim.9), channel_id=1, replica_groups=mesh['y'=4,'z'=12,'core'=2,'y_lo'=2,'x'=4] {'y_lo','x'}, dimensions={0} | all-to-all | bytes 1310720 | tf_op jit(solution)/shard_map/all_to_all | solution.py:22
  43.5 0.3 slice_bitcast_fusion.1
  43.8 0.3 copy.40
  44.1 0.3 copy.41
  44.4 0.6 convolution_convert_fusion.1
  45.0 0.0 copy-start
  45.0 0.0 copy-start.1
  45.0 24.9 %all_to_all.27 = bf16[12,24,512]{2,1,0:T(8,128)(2,1)S(1)} all-to-all(bf16[12,24,512]{2,1,0:T(8,128)(2,1)S(1)} %bitcast.44), channel_id=1, replica_groups=mesh['y'=4,'z'=12,'core'=2,'y_lo'=2,'x'=4] {'z'}, dimensions={0} | all-to-all | bytes 589824 | tf_op jit(solution)/shard_map/all_to_all | solution.py:22
  70.0 0.0 copy-done
  70.0 0.0 copy-done.1
  70.0 0.7 fusion.4
  70.7 17.3 %all_to_all.28 = bf16[12,24,512]{2,1,0:T(8,128)(2,1)S(1)} all-to-all(bf16[12,24,512]{2,1,0:T(8,128)(2,1)S(1)} %broadcast_in_dim.22), channel_id=1, replica_groups=mesh['y'=4,'z'=12,'core'=2,'y_lo'=2,'x'=4] {'z'}, dimensions={0} | all-to-all | bytes 589824 | tf_op jit(solution)/shard_map/all_to_all | solution.py:22
  88.0 0.4 convolution_convert_fusion
  88.4 0.3 copy.42
  88.7 0.1 fusion.9
  88.8 0.1 maximum_maximum_fusion
  88.9 23.5 %all_to_all.29 = bf16[8,184,128]{2,1,0:T(8,128)(2,1)S(1)} all-to-all(bf16[8,184,128]{2,1,0:T(8,128)(2,1)S(1)} %maximum_maximum_fusion), channel_id=1, replica_groups=mesh['y'=4,'z'=12,'core'=2,'y_lo'=2,'x'=4] {'y','core'}, dimensions={0} | all-to-all | bytes 753664 | tf_op jit(solution)/shard_map/all_to_all | solution.py:22
  112.4 0.1 fusion.13
  112.5 0.1 fusion
  112.6 0.3 copy.43
  112.9 0.1 copy.44
  113.0 1.0 copy.45
  (6 shorter events, 0.2 us)
Async XLA Ops:
  2.7 0.7 copy-start.2
  45.0 25.0 %copy-start = (f32[1,24,512]{2,1,0:T(8,128)S(1)}, f32[1,24,512]{2,1,0:T(8,128)}, u32[]{:S(2)}) copy-start(f32[1,24,512]{2,1,0:T(8,128)} %param.8) | copy-start | bytes 147460
  45.0 25.0 %copy-start.1 = (f32[1,24,512]{2,1,0:T(8,128)S(1)}, f32[1,24,512]{2,1,0:T(8,128)}, u32[]{:S(2)}) copy-start(f32[1,24,512]{2,1,0:T(8,128)} %param.7) | copy-start | bytes 147460

commit v3 on v2

v3 whole, which is shorter than its diff:
```python
import math

import jax
import jax.numpy as jnp
from jax import lax
from jax.sharding import PartitionSpec as P

beta_one = 0.9
beta_two = 0.999
adam_eps = 1e-08

SIZES = {"ya": 2, "yb": 2, "za": 2, "zb": 6, "core": 2, "y_lo": 2, "xa": 2, "xb": 2}
FSDP = ("ya", "yb", "za", "zb", "core")
COL = ("y_lo", "xa", "xb")
INNER = ("ya", "yb", "core")
OUTER = ("zb", "za")
OWNERS = ("za", "zb")
LANES = 128


def sizes(axes):
    return tuple(SIZES[axis] for axis in axes)


def order(axes, wanted):
    return tuple(axes.index(axis) for axis in wanted)


N_INNER = math.prod(sizes(INNER))
N_OUTER = math.prod(sizes(OUTER))
N_COL = math.prod(sizes(COL))


def exchange(x, axes):
    return lax.all_to_all(x, axes, split_axis=0, concat_axis=0, tiled=True)


def to_all(x, count):
    return jnp.broadcast_to(x[None], (count,) + x.shape)


def local(grad, basis, exp_avg, exp_avg_sq, step):
    rows, cols = grad.shape
    part = basis.shape[1]
    own, rank = exp_avg.shape[1:]
    wide = cols // N_INNER
    tall = rows * N_INNER
    count = step[0].astype(jnp.float32)
    first_fix = 1.0 - jnp.power(jnp.float32(beta_one), count)
    second_fix = 1.0 - jnp.power(jnp.float32(beta_two), count)
    sent = to_all(basis, N_INNER)
    grad, sent, first_fix, second_fix = lax.optimization_barrier(
        (grad, sent, first_fix, second_fix)
    )

    blocks = grad.reshape((rows,) + sizes(FSDP) + (own,))
    blocks = blocks.transpose(order(("m",) + FSDP + ("k",), INNER + ("m",) + OUTER + ("k",)))
    blocks = blocks.reshape(N_INNER, rows, wide)
    got = exchange(jnp.concatenate([blocks, sent], axis=2), INNER)
    got = got.reshape(tall, wide + part)

    full = exchange(to_all(got[:, wide:].T, N_COL), COL).reshape(rank, tall)

    partial = lax.dot_general(
        got[:, :wide], full, (((0,), (1,)), ((), ())), preferred_element_type=jnp.float32
    )
    sums = exchange(partial.astype(jnp.bfloat16).reshape(N_OUTER, own, rank), OUTER)
    low = jnp.sum(sums.astype(jnp.float32), axis=0).reshape(exp_avg.shape)
    new_avg = beta_one * exp_avg + (1.0 - beta_one) * low
    new_sq = beta_two * exp_avg_sq + (1.0 - beta_two) * low * low
    normalized = (new_avg / first_fix / (jnp.sqrt(new_sq / second_fix) + adam_eps)).astype(
        jnp.bfloat16
    )

    normalized = exchange(to_all(normalized[0], N_OUTER), OWNERS).reshape(wide, rank)
    update = lax.dot_general(
        full, normalized, (((0,), (1,)), ((), ())), preferred_element_type=jnp.float32
    ).astype(jnp.bfloat16)
    update = update.reshape(N_INNER, rows, wide)
    narrow = wide - 2 * LANES
    folds = LANES // narrow
    deep = -(-rows // (8 * folds)) * 8
    tail = jnp.pad(update[:, :, 2 * LANES :], ((0, 0), (0, folds * deep - rows), (0, 0)))
    tail = [tail[:, deep * k : deep * (k + 1)] for k in range(folds)]
    packed = jnp.concatenate(
        [update[:, :, :LANES], update[:, :, LANES : 2 * LANES], jnp.concatenate(tail, axis=2)],
        axis=1,
    )
    packed = exchange(packed, INNER)
    tail = packed[:, 2 * rows :]
    tail = [tail[:, :, narrow * k : narrow * (k + 1)] for k in range(folds)]
    tail = jnp.concatenate(tail, axis=1)[:, :rows]
    update = jnp.concatenate([packed[:, :rows], packed[:, rows : 2 * rows], tail], axis=2)
    update = update.reshape(sizes(INNER) + (rows,) + sizes(OWNERS) + (own,))
    update = update.transpose(order(INNER + ("m",) + OWNERS + ("k",), ("m",) + FSDP + ("k",)))
    return (update.reshape(rows, cols), new_avg, new_sq)


def solution(mesh):
    split = jax.sharding.Mesh(mesh.devices.reshape(sizes(FSDP + COL)), FSDP + COL)
    return jax.shard_map(
        local,
        mesh=split,
        in_specs=(
            P(FSDP, COL),
            P(FSDP, COL),
            P(COL, FSDP, None),
            P(COL, FSDP, None),
            P(),
        ),
        out_specs=(P(FSDP, COL), P(COL, FSDP, None), P(COL, FSDP, None)),
        check_vma=False,
    )
```

time: 114 us -> 114 us (level)
  no operation moved by 1% of the time
where the time goes in v3:
time: 114 us; the launch traced here: 113 us
  blocking collectives  105 us (92%)
  local copies, waits for them, and re-layouts  4.64 us (4%)
  between operations  1.52 us (1%)
    all_to_all x5, blocking collectives, exchange(): return lax.all_to_all(x, axes, split_axis=0, concat_axis=0, tiled=True)  105 us

profile of v3, /device:TPU:1, one launch (start us, length us, event | category | flops | bytes accessed | tf_op | source)
XLA Modules:
  0.0 113.5 jit_solution(15792255929657483758)
XLA Ops:
  1.4 0.7 broadcast_in_dim.8
  2.1 1.3 %copy.38 = bf16[80,2304]{0,1:T(8,128)(2,1)S(1)} copy(bf16[80,2304]{1,0:T(8,128)(2,1)} %param.5) | data formatting | bytes 737280 | tf_op jit(solution)/shard_map/optimization_barrier | solution.py:52
  3.4 0.1 copy.39
  3.5 0.1 pad_maximum_fusion
  3.6 0.3 copy.40
  4.0 26.9 %all_to_all.25 = bf16[8,80,352]{2,1,0:T(8,128)(2,1)S(1)} all-to-all(bf16[8,80,352]{2,1,0:T(8,128)(2,1)S(1)} %copy.40), channel_id=1, replica_groups=mesh['ya'=2,'yb'=2,'za'=2,'zb'=6,'core'=2,'y_lo'=2,'xa'=2,'xb'=2] {'ya',..., dimensions={0} | all-to-all | bytes 901120 | tf_op jit(solution)/shard_map/all_to_all | solution.py:35
  30.9 0.1 slice_bitcast_fusion
  31.0 0.1 copy.41
  31.1 0.1 broadcast_in_dim.9
  31.2 12.4 %all_to_all.26 = bf16[8,64,640]{2,1,0:T(8,128)(2,1)S(1)} all-to-all(bf16[8,64,640]{2,1,0:T(8,128)(2,1)S(1)} %broadcast_in_dim.9), channel_id=1, replica_groups=mesh['ya'=2,'yb'=2,'za'=2,'zb'=6,'core'=2,'y_lo'=2,'xa'=2,'xb'=2] {'y_lo..., dimensions={0} | all-to-all | bytes 1310720 | tf_op jit(solution)/shard_map/all_to_all | solution.py:35
  43.6 0.5 convolution_convert_fusion.1
  44.1 0.0 copy-start
  44.1 0.0 copy-start.1
  44.1 22.9 %all_to_all.27 = bf16[12,24,512]{2,1,0:T(8,128)(2,1)S(1)} all-to-all(bf16[12,24,512]{2,1,0:T(8,128)(2,1)S(1)} %bitcast.41), channel_id=1, replica_groups=mesh['ya'=2,'yb'=2,'za'=2,'zb'=6,'core'=2,'y_lo'=2,'xa'=2,'xb'=2] {'zb',..., dimensions={0} | all-to-all | bytes 589824 | tf_op jit(solution)/shard_map/all_to_all | solution.py:35
  67.0 0.0 copy-done
  67.0 0.0 copy-done.1
  67.0 0.7 fusion.4
  67.7 19.7 %all_to_all.28 = bf16[12,24,512]{2,1,0:T(8,128)(2,1)S(1)} all-to-all(bf16[12,24,512]{2,1,0:T(8,128)(2,1)S(1)} %broadcast_in_dim.22), channel_id=1, replica_groups=mesh['ya'=2,'yb'=2,'za'=2,'zb'=6,'core'=2,'y_lo'=2,'xa'=2,'xb'=2] {'za',..., dimensions={0} | all-to-all | bytes 589824 | tf_op jit(solution)/shard_map/all_to_all | solution.py:35
  87.4 0.4 convolution_convert_fusion
  87.8 0.3 copy.42
  88.1 0.1 fusion.7
  88.2 0.1 maximum_maximum_fusion
  88.3 23.5 %all_to_all.29 = bf16[8,184,128]{2,1,0:T(8,128)(2,1)S(1)} all-to-all(bf16[8,184,128]{2,1,0:T(8,128)(2,1)S(1)} %maximum_maximum_fusion), channel_id=1, replica_groups=mesh['ya'=2,'yb'=2,'za'=2,'zb'=6,'core'=2,'y_lo'=2,'xa'=2,'xb'=2] {'ya',..., dimensions={0} | all-to-all | bytes 753664 | tf_op jit(solution)/shard_map/all_to_all | solution.py:35
  111.9 0.1 fusion.10
  112.0 0.1 fusion
  112.1 0.3 copy.43
  112.4 0.1 copy.44
  112.5 1.0 copy.45
  (5 shorter events, 0.2 us)
Async XLA Ops:
  44.1 23.0 %copy-start = (f32[1,24,512]{2,1,0:T(8,128)S(1)}, f32[1,24,512]{2,1,0:T(8,128)}, u32[]{:S(2)}) copy-start(f32[1,24,512]{2,1,0:T(8,128)} %param.8) | copy-start | bytes 147460
  44.1 23.0 %copy-start.1 = (f32[1,24,512]{2,1,0:T(8,128)S(1)}, f32[1,24,512]{2,1,0:T(8,128)}, u32[]{:S(2)}) copy-start(f32[1,24,512]{2,1,0:T(8,128)} %param.7) | copy-start | bytes 147460

commit v4 on v3

--- a/solution.py
+++ b/solution.py
@@ -14,7 +14,6 @@
 COL = ("y_lo", "xa", "xb")
 INNER = ("ya", "yb", "core")
 OUTER = ("zb", "za")
-OWNERS = ("za", "zb")
 LANES = 128
 
 
@@ -72,7 +71,7 @@
         jnp.bfloat16
     )
 
-    normalized = exchange(to_all(normalized[0], N_OUTER), OWNERS).reshape(wide, rank)
+    normalized = exchange(to_all(normalized[0], N_OUTER), OUTER).reshape(wide, rank)
     update = lax.dot_general(
         full, normalized, (((0,), (1,)), ((), ())), preferred_element_type=jnp.float32
     ).astype(jnp.bfloat16)
@@ -91,8 +90,8 @@
     tail = [tail[:, :, narrow * k : narrow * (k + 1)] for k in range(folds)]
     tail = jnp.concatenate(tail, axis=1)[:, :rows]
     update = jnp.concatenate([packed[:, :rows], packed[:, rows : 2 * rows], tail], axis=2)
-    update = update.reshape(sizes(INNER) + (rows,) + sizes(OWNERS) + (own,))
-    update = update.transpose(order(INNER + ("m",) + OWNERS + ("k",), ("m",) + FSDP + ("k",)))
+    update = update.reshape(sizes(INNER) + (rows,) + sizes(OUTER) + (own,))
+    update = update.transpose(order(INNER + ("m",) + OUTER + ("k",), ("m",) + FSDP + ("k",)))
     return (update.reshape(rows, cols), new_avg, new_sq)
 
 

time: 114 us -> 113 us (level)
  no operation moved by 1% of the time
where the time goes in v4:
time: 113 us; the launch traced here: 112 us
  blocking collectives  104 us (92%)
  local copies, waits for them, and re-layouts  4.64 us (4%)
  between operations  1.52 us (1%)
    all_to_all x5, blocking collectives, exchange(): return lax.all_to_all(x, axes, split_axis=0, concat_axis=0, tiled=True)  104 us

profile of v4, /device:TPU:1, one launch (start us, length us, event | category | flops | bytes accessed | tf_op | source)
XLA Modules:
  0.0 112.5 jit_solution(18417092568360590423)
XLA Ops:
  1.4 0.7 broadcast_in_dim.8
  2.1 1.3 %copy.38 = bf16[80,2304]{0,1:T(8,128)(2,1)S(1)} copy(bf16[80,2304]{1,0:T(8,128)(2,1)} %param.5) | data formatting | bytes 737280 | tf_op jit(solution)/shard_map/optimization_barrier | solution.py:51
  3.4 0.1 copy.39
  3.5 0.1 pad_maximum_fusion
  3.6 0.3 copy.40
  4.0 26.9 %all_to_all.25 = bf16[8,80,352]{2,1,0:T(8,128)(2,1)S(1)} all-to-all(bf16[8,80,352]{2,1,0:T(8,128)(2,1)S(1)} %copy.40), channel_id=1, replica_groups=mesh['ya'=2,'yb'=2,'za'=2,'zb'=6,'core'=2,'y_lo'=2,'xa'=2,'xb'=2] {'ya',..., dimensions={0} | all-to-all | bytes 901120 | tf_op jit(solution)/shard_map/all_to_all | solution.py:34
  30.9 0.1 slice_bitcast_fusion
  31.0 0.1 copy.41
  31.1 0.1 broadcast_in_dim.9
  31.2 12.4 %all_to_all.26 = bf16[8,64,640]{2,1,0:T(8,128)(2,1)S(1)} all-to-all(bf16[8,64,640]{2,1,0:T(8,128)(2,1)S(1)} %broadcast_in_dim.9), channel_id=1, replica_groups=mesh['ya'=2,'yb'=2,'za'=2,'zb'=6,'core'=2,'y_lo'=2,'xa'=2,'xb'=2] {'y_lo..., dimensions={0} | all-to-all | bytes 1310720 | tf_op jit(solution)/shard_map/all_to_all | solution.py:34
  43.6 0.5 convolution_convert_fusion.1
  44.1 0.0 copy-start
  44.1 0.0 copy-start.1
  44.1 22.9 %all_to_all.27 = bf16[12,24,512]{2,1,0:T(8,128)(2,1)S(1)} all-to-all(bf16[12,24,512]{2,1,0:T(8,128)(2,1)S(1)} %bitcast.41), channel_id=1, replica_groups=mesh['ya'=2,'yb'=2,'za'=2,'zb'=6,'core'=2,'y_lo'=2,'xa'=2,'xb'=2] {'zb',..., dimensions={0} | all-to-all | bytes 589824 | tf_op jit(solution)/shard_map/all_to_all | solution.py:34
  67.0 0.0 copy-done
  67.0 0.0 copy-done.1
  67.0 0.7 fusion.4
  67.7 17.7 %all_to_all.28 = bf16[12,24,512]{2,1,0:T(8,128)(2,1)S(1)} all-to-all(bf16[12,24,512]{2,1,0:T(8,128)(2,1)S(1)} %broadcast_in_dim.22), channel_id=1, replica_groups=mesh['ya'=2,'yb'=2,'za'=2,'zb'=6,'core'=2,'y_lo'=2,'xa'=2,'xb'=2] {'zb',..., dimensions={0} | all-to-all | bytes 589824 | tf_op jit(solution)/shard_map/all_to_all | solution.py:34
  85.5 0.4 convolution_convert_fusion
  85.9 0.3 copy.42
  86.2 0.1 fusion.7
  86.3 0.1 maximum_maximum_fusion
  86.4 24.5 %all_to_all.29 = bf16[8,184,128]{2,1,0:T(8,128)(2,1)S(1)} all-to-all(bf16[8,184,128]{2,1,0:T(8,128)(2,1)S(1)} %maximum_maximum_fusion), channel_id=1, replica_groups=mesh['ya'=2,'yb'=2,'za'=2,'zb'=6,'core'=2,'y_lo'=2,'xa'=2,'xb'=2] {'ya',..., dimensions={0} | all-to-all | bytes 753664 | tf_op jit(solution)/shard_map/all_to_all | solution.py:34
  110.9 0.1 fusion.10
  111.0 0.1 fusion
  111.1 0.3 copy.43
  111.4 0.1 copy.44
  111.5 1.0 copy.45
  (5 shorter events, 0.2 us)
Async XLA Ops:
  44.1 23.0 %copy-start = (f32[1,24,512]{2,1,0:T(8,128)S(1)}, f32[1,24,512]{2,1,0:T(8,128)}, u32[]{:S(2)}) copy-start(f32[1,24,512]{2,1,0:T(8,128)} %param.8) | copy-start | bytes 147460
  44.1 23.0 %copy-start.1 = (f32[1,24,512]{2,1,0:T(8,128)S(1)}, f32[1,24,512]{2,1,0:T(8,128)}, u32[]{:S(2)}) copy-start(f32[1,24,512]{2,1,0:T(8,128)} %param.7) | copy-start | bytes 147460

commit v5 on v4

--- a/solution.py
+++ b/solution.py
@@ -12,7 +12,7 @@
 SIZES = {"ya": 2, "yb": 2, "za": 2, "zb": 6, "core": 2, "y_lo": 2, "xa": 2, "xb": 2}
 FSDP = ("ya", "yb", "za", "zb", "core")
 COL = ("y_lo", "xa", "xb")
-INNER = ("ya", "yb", "core")
+INNER = ("yb", "ya", "core")
 OUTER = ("zb", "za")
 LANES = 128
 

time: 113 us -> 113 us (level)
  no operation moved by 1% of the time
where the time goes in v5:
time: 113 us; the launch traced here: 112 us
  blocking collectives  104 us (92%)
  local copies, waits for them, and re-layouts  4.64 us (4%)
  between operations  1.52 us (1%)
    all_to_all x5, blocking collectives, exchange(): return lax.all_to_all(x, axes, split_axis=0, concat_axis=0, tiled=True)  104 us

profile of v5, /device:TPU:1, one launch (start us, length us, event | category | flops | bytes accessed | tf_op | source)
XLA Modules:
  0.0 112.1 jit_solution(13488007389078185630)
XLA Ops:
  1.4 0.7 broadcast_in_dim.8
  2.1 1.3 %copy.38 = bf16[80,2304]{0,1:T(8,128)(2,1)S(1)} copy(bf16[80,2304]{1,0:T(8,128)(2,1)} %param.5) | data formatting | bytes 737280 | tf_op jit(solution)/shard_map/optimization_barrier | solution.py:51
  3.4 0.1 copy.39
  3.5 0.1 pad_maximum_fusion
  3.6 0.3 copy.40
  4.0 25.0 %all_to_all.25 = bf16[8,80,352]{2,1,0:T(8,128)(2,1)S(1)} all-to-all(bf16[8,80,352]{2,1,0:T(8,128)(2,1)S(1)} %copy.40), channel_id=1, replica_groups=mesh['ya'=2,'yb'=2,'za'=2,'zb'=6,'core'=2,'y_lo'=2,'xa'=2,'xb'=2] {'yb',..., dimensions={0} | all-to-all | bytes 901120 | tf_op jit(solution)/shard_map/all_to_all | solution.py:34
  29.0 0.1 slice_bitcast_fusion
  29.1 0.1 copy.41
  29.2 0.1 broadcast_in_dim.9
  29.3 12.5 %all_to_all.26 = bf16[8,64,640]{2,1,0:T(8,128)(2,1)S(1)} all-to-all(bf16[8,64,640]{2,1,0:T(8,128)(2,1)S(1)} %broadcast_in_dim.9), channel_id=1, replica_groups=mesh['ya'=2,'yb'=2,'za'=2,'zb'=6,'core'=2,'y_lo'=2,'xa'=2,'xb'=2] {'y_lo..., dimensions={0} | all-to-all | bytes 1310720 | tf_op jit(solution)/shard_map/all_to_all | solution.py:34
  41.7 0.5 convolution_convert_fusion.1
  42.2 0.0 copy-start
  42.3 0.0 copy-start.1
  42.3 24.2 %all_to_all.27 = bf16[12,24,512]{2,1,0:T(8,128)(2,1)S(1)} all-to-all(bf16[12,24,512]{2,1,0:T(8,128)(2,1)S(1)} %bitcast.41), channel_id=1, replica_groups=mesh['ya'=2,'yb'=2,'za'=2,'zb'=6,'core'=2,'y_lo'=2,'xa'=2,'xb'=2] {'zb',..., dimensions={0} | all-to-all | bytes 589824 | tf_op jit(solution)/shard_map/all_to_all | solution.py:34
  66.5 0.0 copy-done
  66.6 0.0 copy-done.1
  66.6 0.7 fusion.4
  67.3 18.7 %all_to_all.28 = bf16[12,24,512]{2,1,0:T(8,128)(2,1)S(1)} all-to-all(bf16[12,24,512]{2,1,0:T(8,128)(2,1)S(1)} %broadcast_in_dim.22), channel_id=1, replica_groups=mesh['ya'=2,'yb'=2,'za'=2,'zb'=6,'core'=2,'y_lo'=2,'xa'=2,'xb'=2] {'zb',..., dimensions={0} | all-to-all | bytes 589824 | tf_op jit(solution)/shard_map/all_to_all | solution.py:34
  85.9 0.4 convolution_convert_fusion
  86.3 0.3 copy.42
  86.6 0.1 fusion.7
  86.7 0.1 maximum_maximum_fusion
  86.9 23.6 %all_to_all.29 = bf16[8,184,128]{2,1,0:T(8,128)(2,1)S(1)} all-to-all(bf16[8,184,128]{2,1,0:T(8,128)(2,1)S(1)} %maximum_maximum_fusion), channel_id=1, replica_groups=mesh['ya'=2,'yb'=2,'za'=2,'zb'=6,'core'=2,'y_lo'=2,'xa'=2,'xb'=2] {'yb',..., dimensions={0} | all-to-all | bytes 753664 | tf_op jit(solution)/shard_map/all_to_all | solution.py:34
  110.5 0.1 fusion.10
  110.6 0.1 fusion
  110.7 0.3 copy.43
  111.0 0.1 copy.44
  111.1 1.0 copy.45
  (5 shorter events, 0.2 us)
Async XLA Ops:
  42.2 24.3 %copy-start = (f32[1,24,512]{2,1,0:T(8,128)S(1)}, f32[1,24,512]{2,1,0:T(8,128)}, u32[]{:S(2)}) copy-start(f32[1,24,512]{2,1,0:T(8,128)} %param.8) | copy-start | bytes 147460
  42.3 24.3 %copy-start.1 = (f32[1,24,512]{2,1,0:T(8,128)S(1)}, f32[1,24,512]{2,1,0:T(8,128)}, u32[]{:S(2)}) copy-start(f32[1,24,512]{2,1,0:T(8,128)} %param.7) | copy-start | bytes 147460
